TPU v7x, 32 devices: a whole 2x2x4 slice. The times are simulated.
32 devices in a mesh: dp: 16 (over z, x, core), seq: 2 (over y).
Axes of the slice: x: 2, y: 2, z: 4, core: 2. Of those that a mesh axis runs over, the one named last changes fastest.
Arguments:
- tokens: bfloat16 [64, 512, 768], P('dp', 'seq'), may hold values from -6 to 6
- weight_in: bfloat16 [768, 3072], P(('dp', 'seq')), may hold values from -0.21875 to 0.21875
- bias_in: bfloat16 [3072], P(('dp', 'seq')), may hold values from -3 to 3
- weight_out: bfloat16 [3072, 768], P(('dp', 'seq')), may hold values from -0.15625 to 0.15625
- bias_out: bfloat16 [768], P(('dp', 'seq')), may hold values from -2 to 2
- gain_mix: bfloat16 [768], P(('dp', 'seq')), may hold values from 0.099609375 to 1.8984375
- shift_mix: bfloat16 [768], P(('dp', 'seq')), may hold values from -2 to 2
- gain_ffn: bfloat16 [768], P(('dp', 'seq')), may hold values from 0.099609375 to 1.8984375
- shift_ffn: bfloat16 [768], P(('dp', 'seq')), may hold values from -2 to 2
- cotangent: bfloat16 [64, 512, 768], P('dp', 'seq'), may hold values from -6 to 6
Outputs:
- output: bfloat16 [64, 512, 768], P('dp', 'seq')
- grad_tokens: float32 [64, 512, 768], P('dp', 'seq')
- grad_weight_in: float32 [768, 3072], P(('dp', 'seq'))
- grad_bias_in: float32 [3072], P(('dp', 'seq'))
- grad_weight_out: float32 [3072, 768], P(('dp', 'seq'))
- grad_bias_out: float32 [768], P(('dp', 'seq'))
- grad_gain_mix: float32 [768], P(('dp', 'seq'))
- grad_shift_mix: float32 [768], P(('dp', 'seq'))
- grad_gain_ffn: float32 [768], P(('dp', 'seq'))
- grad_shift_ffn: float32 [768], P(('dp', 'seq'))
All inputs are finite; a program needn't handle non-finite values.
Results may differ from a plain program's by a relative error of at most 0.0074.
Values may be sent and summed in bfloat16 or wider, within the bound.
No kernel may reach another device: no remote copies, remote signals or barrier semaphores. Data moves between devices by JAX's collectives and lax.ppermute only.
A program may use at most 192 MiB of HBM per device.

v0:
```python
import math
import jax
import jax.numpy as jnp
from jax import lax
from jax.sharding import PartitionSpec as P

EPS = 1e-12


def dft_block(row_start, row_count, col_start, col_count, length):
    row_index = row_start + lax.iota(jnp.int32, row_count)
    col_index = col_start + lax.iota(jnp.int32, col_count)
    product = row_index[:, None] * col_index[None, :] % length
    angle = product.astype(jnp.float32) * (2.0 * math.pi / length)
    scale = length ** (-0.5)
    return (jnp.cos(angle) * scale, jnp.sin(angle) * scale)


def layer_norm(values, gain, shift):
    center = values - jnp.mean(values, axis=-1, keepdims=True)
    spread = jnp.mean(center * center, axis=-1, keepdims=True)
    return center * lax.rsqrt(spread + EPS) * gain + shift


def gelu_exact(values):
    return jax.nn.gelu(values, approximate=False)


def per_device(
    tokens,
    weight_in,
    bias_in,
    weight_out,
    bias_out,
    gain_mix,
    shift_mix,
    gain_ffn,
    shift_ffn,
    cotangent,
):
    gathered = (
        lax.all_gather(weight_in, ("dp", "seq"), axis=0, tiled=True),
        lax.all_gather(bias_in, ("dp", "seq"), axis=0, tiled=True),
        lax.all_gather(weight_out, ("dp", "seq"), axis=0, tiled=True),
        lax.all_gather(bias_out, ("dp", "seq"), axis=0, tiled=True),
        lax.all_gather(gain_mix, ("dp", "seq"), axis=0, tiled=True),
        lax.all_gather(shift_mix, ("dp", "seq"), axis=0, tiled=True),
        lax.all_gather(gain_ffn, ("dp", "seq"), axis=0, tiled=True),
        lax.all_gather(shift_ffn, ("dp", "seq"), axis=0, tiled=True),
    )
    full_w_in, full_b_in, full_w_out, full_b_out = (
        gathered[0],
        gathered[1],
        gathered[2],
        gathered[3],
    )
    mix_gain = gathered[4].astype(jnp.float32)
    mix_shift = gathered[5].astype(jnp.float32)
    ffn_gain = gathered[6].astype(jnp.float32)
    ffn_shift = gathered[7].astype(jnp.float32)
    rows, block_len, width = tokens.shape
    length = block_len * lax.axis_size("seq")
    my_start = lax.axis_index("seq") * block_len
    piece = lax.all_gather(tokens, "seq", axis=1, tiled=True)
    cos_part, sin_part = dft_block(my_start, block_len, jnp.int32(0), piece.shape[1], length)
    table = jnp.concatenate([cos_part, sin_part], axis=0).astype(jnp.bfloat16)
    stacked = jnp.einsum("kn,rnd->rkd", table, piece, preferred_element_type=jnp.float32)
    spectra = jnp.concatenate([stacked[:, :block_len], stacked[:, block_len:]], axis=-1).astype(
        jnp.bfloat16
    )
    cos_hid, sin_hid = dft_block(0, width, 0, width, width)
    hid_table = jnp.concatenate([cos_hid, -sin_hid], axis=0).astype(jnp.bfloat16)
    mixed = jnp.einsum("rkj,jd->rkd", spectra, hid_table, preferred_element_type=jnp.float32)
    resid_one = tokens.astype(jnp.float32) + mixed
    normed, norm_pull = jax.vjp(layer_norm, resid_one, mix_gain, mix_shift)
    normed_low = normed.astype(jnp.bfloat16)
    hidden_pre = jnp.einsum(
        "rkd,df->rkf", normed_low, full_w_in, preferred_element_type=jnp.float32
    ) + full_b_in.astype(jnp.float32)
    activated, gelu_pull = jax.vjp(gelu_exact, hidden_pre)
    act_low = activated.astype(jnp.bfloat16)
    branch = jnp.einsum(
        "rkf,fd->rkd", act_low, full_w_out, preferred_element_type=jnp.float32
    ) + full_b_out.astype(jnp.float32)
    result, final_pull = jax.vjp(layer_norm, normed + branch, ffn_gain, ffn_shift)
    d_resid_two, d_gain_ffn, d_shift_ffn = final_pull(cotangent.astype(jnp.float32))
    d_branch = d_resid_two.astype(jnp.bfloat16)
    grad_w_out = jnp.einsum("rkf,rkd->fd", act_low, d_branch, preferred_element_type=jnp.float32)
    grad_b_out = jnp.sum(d_branch.astype(jnp.float32), axis=(0, 1))
    d_act = jnp.einsum("rkd,fd->rkf", d_branch, full_w_out, preferred_element_type=jnp.float32)
    (d_pre,) = gelu_pull(d_act)
    d_pre_low = d_pre.astype(jnp.bfloat16)
    grad_w_in = jnp.einsum("rkd,rkf->df", normed_low, d_pre_low, preferred_element_type=jnp.float32)
    grad_b_in = jnp.sum(d_pre_low.astype(jnp.float32), axis=(0, 1))
    d_normed = d_resid_two + jnp.einsum(
        "rkf,df->rkd", d_pre_low, full_w_in, preferred_element_type=jnp.float32
    )
    d_resid_one, d_gain_mix, d_shift_mix = norm_pull(d_normed)
    d_mix_low = d_resid_one.astype(jnp.bfloat16)
    d_spectra = jnp.einsum(
        "rkd,jd->rkj", d_mix_low, hid_table, preferred_element_type=jnp.float32
    ).astype(jnp.bfloat16)
    piece = lax.all_gather(d_spectra, "seq", axis=1, tiled=True)
    count = piece.shape[1]
    cos_part, sin_part = dft_block(jnp.int32(0), count, my_start, block_len, length)
    table = jnp.stack([cos_part, sin_part], axis=0).astype(jnp.bfloat16)
    halves = piece.reshape(rows, count, 2, width)
    d_tokens_mix = jnp.einsum("ckn,rkcd->rnd", table, halves, preferred_element_type=jnp.float32)
    grad_tokens = d_resid_one + d_tokens_mix
    reduced = (
        lax.psum_scatter(grad_w_in, ("dp", "seq"), scatter_dimension=0, tiled=True),
        lax.psum_scatter(grad_b_in, ("dp", "seq"), scatter_dimension=0, tiled=True),
        lax.psum_scatter(grad_w_out, ("dp", "seq"), scatter_dimension=0, tiled=True),
        lax.psum_scatter(grad_b_out, ("dp", "seq"), scatter_dimension=0, tiled=True),
        lax.psum_scatter(d_gain_mix, ("dp", "seq"), scatter_dimension=0, tiled=True),
        lax.psum_scatter(d_shift_mix, ("dp", "seq"), scatter_dimension=0, tiled=True),
        lax.psum_scatter(d_gain_ffn, ("dp", "seq"), scatter_dimension=0, tiled=True),
        lax.psum_scatter(d_shift_ffn, ("dp", "seq"), scatter_dimension=0, tiled=True),
    )
    return (
        result.astype(jnp.bfloat16),
        grad_tokens,
        reduced[0],
        reduced[1],
        reduced[2],
        reduced[3],
        reduced[4],
        reduced[5],
        reduced[6],
        reduced[7],
    )


def solution(mesh):
    in_specs = (
        P("dp", "seq", None),
        P(("dp", "seq"), None),
        P(("dp", "seq")),
        P(("dp", "seq"), None),
        P(("dp", "seq")),
        P(("dp", "seq")),
        P(("dp", "seq")),
        P(("dp", "seq")),
        P(("dp", "seq")),
        P("dp", "seq", None),
    )
    out_specs = (
        P("dp", "seq", None),
        P("dp", "seq", None),
        P(("dp", "seq"), None),
        P(("dp", "seq")),
        P(("dp", "seq"), None),
        P(("dp", "seq")),
        P(("dp", "seq")),
        P(("dp", "seq")),
        P(("dp", "seq")),
        P(("dp", "seq")),
    )
    return jax.shard_map(
        per_device, mesh=mesh, in_specs=in_specs, out_specs=out_specs, check_vma=False
    )
```

profile of v0, /device:TPU:0, one launch (start us, length us, event | category | flops | bytes accessed | tf_op | source)
XLA Modules:
  0.0 613.3 jit_solution(7651262054729661648)
XLA Ops:
  7.3 0.7 all-gather.5.cloned.1.call-update
  8.0 0.7 all-gather.7.cloned.1.call-update
  9.5 10.7 %negate_convert_fusion = (bf16[768,768]{1,0:T(8,128)(2,1)}, bf16[768,768]{1,0:T(8,128)(2,1)}) fusion(), kind=kLoop, calls=%fused_computation.66 | loop fusion | flops 8257536 | bytes 2359296 | tf_op jit(solution)/shard_map/convert.3
  21.7 42.5 %all-reduce.13 = (bf16[768]{0:T(1024)(128)(2,1)S(1)}, bf16[768]{0:T(1024)(128)(2,1)S(1)}, bf16[3072]{0:T(1024)(128)(2,1)S(1)}, bf16[768]{0:T(1024)(128)(2,1)S(1)...) all-reduce(bf16[768]{0:T(1024)(128)(2,1)S(1)} %dynamic-update-slice, ...), channel_id=1, replica_groups=mesh['dp'=16,'seq'=2] {'dp','seq'}, use_global_device_ids=true, to_apply=%add.1 | all-reduce | flops 6912 | bytes 27648
  64.2 3.0 multiply_convert_fusion.5
  67.2 3.7 convert_bitcast_fusion
  71.2 1.2 copy-done.4
  73.1 2.8 fusion.64
  76.4 48.4 %all-gather.7.cloned.1.call-done = bf16[768,3072]{1,0:T(8,128)(2,1)} async-done(((bf16[24,3072]{1,0:T(8,128)(2,1)}), bf16[768,3072]{1,0:T(8,128)(2,1)}) %all-gather.7.cloned.1.call-update) | async-done | bytes 4718608 | tf_op jit(solution)/shard_map/all_gather | solution.py:42
  124.8 10.8 %fusion.22 = (u8[256,3072]{1,0:T(8,128)(4,1)S(1)}, u8[256,3072]{1,0:T(8,128)(4,1)S(1)}, f32[4,256,3072]{2,1,0:T(8,128)S(1)}) fusion(f32[3072]{0:T(1024)S(1)} %convert_element_type.83, bf16[768,3072]{1,0:T(8,128)(2,1)} %all-gather.7.cloned.1.call-done, f32[4,256,768]{2,1,0:T(8,128)S(1)} %get-tuple-element.48, f32[768]{0:T(1024)S(1)} %convert_element_type.81, ...), kind=kOutput, calls=%fused_computation.58 | convolution fusion | flops 4878237696 | bytes 22046720 | tf_op jit(solution)/shard_map/rkd,df->rkf/dot_general | solution.py:77
  135.6 4.5 copy-done.1
  140.0 30.4 %multiply_convert_fusion = (bf16[4,256,3072]{2,1,0:T(8,128)(2,1)}, f32[4,256,3072]{2,1,0:T(8,128)}) fusion(f32[4,256,3072]{2,1,0:T(8,128)S(1)} %get-tuple-element.49, f32[3072]{0:T(1024)S(1)} %convert_element_type.83, u8[256,3072]{1,0:T(8,128)(4,1)S(1)} %get-tuple-element.11, u8[256,3072]{1,0:T(8,128)(4,1)S(1)} %get-tuple-element.10), kind=kLoop, calls=%fused_computation.9 | loop fusion | flops 223346688 | bytes 33042432 | tf_op jit(solution)/shard_map/convert_element_type | solution.py:81
  170.5 19.7 %all-gather.9.cloned.1.call-done = bf16[3072,768]{1,0:T(8,128)(2,1)} async-done(((bf16[96,768]{1,0:T(8,128)(2,1)}), bf16[3072,768]{1,0:T(8,128)(2,1)}) %all-gather.9.cloned.1.call-update) | async-done | bytes 4718608 | tf_op jit(solution)/shard_map/all_gather | solution.py:44
  190.2 8.9 %fusion.65 = (f32[4,256]{1,0:T(4,128)S(1)}, f32[4,256,768]{2,1,0:T(8,128)S(1)}) fusion(f32[768]{0:T(1024)S(1)} %convert_element_type.85, bf16[4,256,3072]{2,1,0:T(8,128)(2,1)} %get-tuple-element.36, bf16[3072,768]{1,0:T(8,128)(2,1)} %all-gather.9.cloned.1.call-done, f32[768]{0:T(1024)S(1)} %convert_element_type.81, f32[768]{0:T(1024)S(1)} %convert_element_type.80, ...), kind=kOutput, calls=%fused_computation.120 | convolution fusion | flops 4837342208 | bytes 17323008 | tf_op jit(solution)/shard_map/rkf,fd->rkd/dot_general | solution.py:82
  199.2 1.4 fusion.15
  200.6 1.8 fusion.16
  202.4 2.7 convert_reduce_fusion.2
  205.1 18.1 %convert_reduce_fusion = (f32[3072]{0:T(1024)S(1)}, bf16[4,256,3072]{2,1,0:T(8,128)(2,1)}) fusion(f32[4,256,3072]{2,1,0:T(8,128)} %get-tuple-element.37, bf16[4,256,768]{2,1,0:T(8,128)(2,1)} %get-tuple-element.33, bf16[3072,768]{1,0:T(8,128)(2,1)} %all-gather.9.cloned.1.call-done, f32[4,256,3072]{2,1,0:T(8,128)} %copy-done.1, f32[3072]{0:T(1024)S(1)} %convert_element_type.83), kind=kOutput, calls=%fused_computation.7 | convolution fusion | flops 4885312512 | bytes 37773312 | tf_op jit(solution)/shard_map/rkd,fd->rkf/dot_general | solution.py:90
  223.3 10.3 %multiply_reduce_fusion = (f32[768]{0:T(1024)S(1)}, f32[4,256]{1,0:T(4,128)S(1)}, f32[768]{0:T(1024)S(1)}, f32[4,256,768]{2,1,0:T(8,128)S(1)}) fusion(f32[4,256,768]{2,1,0:T(8,128)S(1)} %get-tuple-element.48, f32[4,256]{1,0:T(4,128)S(1)} %fusion.54, f32[4,256]{1,0:T(4,128)S(1)} %broadcast_multiply_fusion.1, f32[768]{0:T(1024)S(1)} %convert_element_type.80, ...), kind=kOutput, calls=%fused_computation.48 | convolution fusion | flops 4845204480 | bytes 22061056 | tf_op jit(solution)/shard_map/rkf,df->rkd/dot_general | solution.py:95
  233.6 1.2 fusion.61
  234.9 1.6 copy-done.2
  236.5 5.0 convolution_convert_fusion
  241.6 10.6 %convolution_bitcast_fusion.1 = f32[768,3072]{1,0:T(8,128)} fusion(bf16[4,256,3072]{2,1,0:T(8,128)(2,1)} %get-tuple-element.54, f32[4,256,768]{2,1,0:T(8,128)S(1)} %get-tuple-element.48, f32[768]{0:T(1024)S(1)} %convert_element_type.81, f32[768]{0:T(1024)S(1)} %convert_element_type.80, f32[4,256]{1,0:T(4,128)S(1)} %fusion.54, ...), kind=kOutput, calls=%fused_computation.23 | convolution fusion | flops 4835770368 | bytes 18888704 | tf_op jit(solution)/shard_map/rkd,rkf->df/dot_general | solution.py:93
  252.3 1.5 copy-done.5
  253.8 10.7 %convolution_bitcast_fusion = f32[3072,768]{1,0:T(8,128)} fusion(bf16[4,256,3072]{2,1,0:T(8,128)(2,1)} %get-tuple-element.36, bf16[4,256,768]{2,1,0:T(8,128)(2,1)S(1)} %copy-done.5), kind=kOutput, calls=%fused_computation.22 | convolution fusion | flops 4831838208 | bytes 17301504 | tf_op jit(solution)/shard_map/rkf,rkd->fd/dot_general | solution.py:88
  264.5 3.0 multiply_convert_fusion.3
  267.5 40.9 %all-reduce.12 = (f32[3072]{0:T(1024)S(1)}, f32[768]{0:T(1024)S(1)}, f32[768]{0:T(1024)S(1)}, f32[768]{0:T(1024)S(1)}, f32[768]{0:T(1024)S(1)}, /*index=5*/f32[768]{0:T(1024)S(1)}) all-reduce(f32[3072]{0:T(1024)S(1)} %get-tuple-element.53, f32[768]{0:T(1024)S(1)} %get-tuple-element.32, ...), channel_id=3, replica_groups=mesh['dp'=16,'seq'=2] {'dp','seq'}, use_global_device_ids=true, to_apply=%region_10.11.clone | all-reduce | flops 6912 | bytes 55296
  311.9 10.4 %all-gather.11.cloned.1.call-done = bf16[4,512,1536]{2,1,0:T(8,128)(2,1)} async-done(((bf16[4,256,1536]{2,1,0:T(8,128)(2,1)}), bf16[4,512,1536]{2,1,0:T(8,128)(2,1)}) %all-gather.11.cloned.1.call-update) | async-done | bytes 6291472 | tf_op jit(solution)/shard_map/all_gather | solution.py:103
  322.3 8.6 %copy.31 = bf16[4,512,1536]{1,2,0:T(8,128)(2,1)} copy(bf16[4,512,1536]{2,1,0:T(8,128)(2,1)} %all-gather.11.cloned.1.call-done) | data formatting | bytes 12582912 | tf_op jit(solution)/shard_map/reshape | solution.py:107
  330.9 6.3 %bitcast_add_fusion = f32[4,256,768]{2,1,0:T(8,128)} fusion(f32[4,256,768]{2,1,0:T(8,128)S(1)} %copy-done.3, bf16[4,512,2,768]{1,3,2,0:T(8,128)(2,1)} %bitcast.53, f32[4,256]{1,0:T(4,128)S(1)} %negate_multiply_fusion.1, bf16[1,512,256]{2,1,0:T(8,128)(2,1)} %get-tuple-element.44, bf16[1,512,256]{2,1,0:T(8,128)(2,1)S(1)} %get-tuple-element.43), kind=kOutput, calls=%fused_computation.46 | convolution fusion | flops 1612447744 | bytes 13111296 | tf_op jit(solution)/shard_map/ckn,rkcd->rnd/dot_general | solution.py:108
  337.2 126.8 %reduce-scatter.3.cloned.1.call-done = f32[24,3072]{1,0:T(8,128)} async-done(((f32[768,3072]{1,0:T(8,128)}), f32[24,3072]{1,0:T(8,128)}) %reduce-scatter.3.cloned.1.call-update) | async-done | bytes 294928 | tf_op jit(solution)/shard_map/reduce_scatter | solution.py:111
  464.0 142.2 %reduce-scatter.5.cloned.1.call-done = f32[96,768]{1,0:T(8,128)} async-done(((f32[3072,768]{1,0:T(8,128)}), f32[96,768]{1,0:T(8,128)}) %reduce-scatter.5.cloned.1.call-update) | async-done | bytes 294928 | tf_op jit(solution)/shard_map/reduce_scatter | solution.py:113
  (73 shorter events, 7.4 us)
Async XLA Ops:
  7.2 13.1 %copy-start.10 = (bf16[24]{0:T(256)(128)(2,1)S(1)}, bf16[24]{0:T(256)(128)(2,1)}, u32[]{:S(2)}) copy-start(bf16[24]{0:T(256)(128)(2,1)} %param.16) | copy-start | bytes 148
  7.2 13.3 %copy-start.11 = (bf16[24]{0:T(256)(128)(2,1)S(1)}, bf16[24]{0:T(256)(128)(2,1)}, u32[]{:S(2)}) copy-start(bf16[24]{0:T(256)(128)(2,1)} %param.15) | copy-start | bytes 148
  7.2 13.5 %copy-start.12 = (bf16[24]{0:T(256)(128)(2,1)S(1)}, bf16[24]{0:T(256)(128)(2,1)}, u32[]{:S(2)}) copy-start(bf16[24]{0:T(256)(128)(2,1)} %param.14) | copy-start | bytes 148
  7.2 13.8 %copy-start.13 = (bf16[24]{0:T(256)(128)(2,1)S(1)}, bf16[24]{0:T(256)(128)(2,1)}, u32[]{:S(2)}) copy-start(bf16[24]{0:T(256)(128)(2,1)} %param.18) | copy-start | bytes 148
  7.2 14.0 %copy-start.14 = (bf16[24]{0:T(256)(128)(2,1)S(1)}, bf16[24]{0:T(256)(128)(2,1)}, u32[]{:S(2)}) copy-start(bf16[24]{0:T(256)(128)(2,1)} %param.17) | copy-start | bytes 148
  7.2 14.2 %copy-start.15 = (bf16[96]{0:T(256)(128)(2,1)S(1)}, bf16[96]{0:T(256)(128)(2,1)}, u32[]{:S(2)}) copy-start(bf16[96]{0:T(256)(128)(2,1)} %param.12) | copy-start | bytes 580
  7.2 60.0 %all-gather.5.cloned.1.call-start = ((), (), s32[]{:S(2)}) async-start(), calls=%async_computation.2 | async-start | bytes 4718592 | tf_op jit(solution)/shard_map/all_gather | solution.py:64
  8.0 116.8 %all-gather.7.cloned.1.call-start = ((), (), s32[]{:S(2)}) async-start(), calls=%async_computation.3 | async-start | bytes 4866048 | tf_op jit(solution)/shard_map/all_gather | solution.py:42
  8.7 181.5 %all-gather.9.cloned.1.call-start = ((), (), s32[]{:S(2)}) async-start(), calls=%async_computation.4 | async-start | bytes 4866048 | tf_op jit(solution)/shard_map/all_gather | solution.py:44
  9.5 312.8 %all-gather.11.cloned.1.call-start = ((), (), s32[]{:S(2)}) async-start(), calls=%async_computation.5 | async-start | bytes 9437184 | tf_op jit(solution)/shard_map/all_gather | solution.py:103
  71.0 1.4 copy-start.4
  71.0 1.7 copy-start.6
  71.0 2.1 copy-start.8
  135.6 4.5 copy-start.1
  190.2 8.9 %copy-start = (bf16[4,256,768]{2,1,0:T(8,128)(2,1)S(1)}, bf16[4,256,768]{2,1,0:T(8,128)(2,1)}, u32[]{:S(2)}) copy-start(bf16[4,256,768]{2,1,0:T(8,128)(2,1)} %param.19) | copy-start | bytes 4718596
  233.6 2.9 copy-start.7
  233.6 2.9 copy-start.9
  234.8 1.7 copy-start.2
  241.5 222.5 %reduce-scatter.3.cloned.1.call-start = ((), (), s32[]{:S(2)}) async-start(), calls=%async_computation.6 | async-start | bytes 9732096 | tf_op jit(solution)/shard_map/reduce_scatter | solution.py:111
  252.2 1.6 copy-start.5
  252.2 354.0 %reduce-scatter.5.cloned.1.call-start = ((), (), s32[]{:S(2)}) async-start(), calls=%async_computation.7 | async-start | bytes 9732096 | tf_op jit(solution)/shard_map/reduce_scatter | solution.py:113
  311.9 19.0 %copy-start.3 = (f32[4,256,768]{2,1,0:T(8,128)S(1)}, f32[4,256,768]{2,1,0:T(8,128)}, u32[]{:S(2)}) copy-start(f32[4,256,768]{2,1,0:T(8,128)} %copy-done.2) | copy-start | bytes 9437188
Sparse Core Ops, SparseCore 0:
  9.6 48.4 all-gather.4
  61.0 63.7 all-gather.6
  127.7 62.4 all-gather.8
  241.6 80.5 all-gather.10
  328.6 135.3 reduce-scatter.2
  471.3 134.8 reduce-scatter.4
where the time goes:
time: 617 us; the launch traced here: 613 us
  waiting for transfers between devices  350 us (57%)
  matrix products  87.3 us (14%)
  blocking collectives  83.4 us (14%)
  other arithmetic  54.9 us (9%)
  local copies, waits for them, and re-layouts  23.2 us (4%)
  between operations  14.7 us (2%)
    reduce_scatter x1, waiting for transfers between devices, per_device(): lax.psum_scatter(grad_w_out, ('dp', 'seq'), scatter_dimension=0, tiled=True)  142 us
    reduce_scatter x1, waiting for transfers between devices, per_device(): lax.psum_scatter(grad_w_in, ('dp', 'seq'), scatter_dimension=0, tiled=True)  127 us
    unnamed x2, blocking collectives  83.4 us
    all_gather x1, waiting for transfers between devices, per_device(): lax.all_gather(weight_in, ('dp', 'seq'), axis=0, tiled=True)  48.4 us
    convert_element_type x1, other arithmetic, per_device(): act_low = activated.astype(jnp.bfloat16)  30.4 us
    all_gather x1, waiting for transfers between devices, per_device(): lax.all_gather(weight_out, ('dp', 'seq'), axis=0, tiled=True)  19.7 us
    dot_general x1, matrix products, per_device(): jnp.einsum('rkd,fd->rkf', d_branch, full_w_out, preferred_element_type=jn...  18.1 us
    another operation x3, other arithmetic  16.7 us
  transfers between devices with their start and end apart: 6, of which 5 were waited for; matrix products, arithmetic and copies ran while one was open for 17% of the time, Pallas kernels for 0%

commit v1 on v0

--- a/solution.py
+++ b/solution.py
@@ -5,6 +5,18 @@
 from jax.sharding import PartitionSpec as P
 
 EPS = 1e-12
+
+
+def collect(shard, axis, dim):
+    ways, here = (lax.axis_size(axis), lax.axis_index(axis))
+    grown, reach = (shard, 1)
+    while reach < ways:
+        theirs = lax.ppermute(grown, axis, [(d, d ^ reach) for d in range(ways)])
+        mine_first = jnp.concatenate([grown, theirs], axis=dim)
+        theirs_first = jnp.concatenate([theirs, grown], axis=dim)
+        grown = jnp.where(here & reach == 0, mine_first, theirs_first)
+        reach = 2 * reach
+    return grown
 
 
 def dft_block(row_start, row_count, col_start, col_count, length):
@@ -39,7 +51,7 @@
     cotangent,
 ):
     gathered = (
-        lax.all_gather(weight_in, ("dp", "seq"), axis=0, tiled=True),
+        collect(weight_in, ("dp", "seq"), 0),
         lax.all_gather(bias_in, ("dp", "seq"), axis=0, tiled=True),
         lax.all_gather(weight_out, ("dp", "seq"), axis=0, tiled=True),
         lax.all_gather(bias_out, ("dp", "seq"), axis=0, tiled=True),

time: 617 us -> 679 us (1.10)
  blocking collectives: 83.4 us -> 164 us
  waiting for transfers between devices: 350 us -> 315 us
  starting transfers between devices: 0.23 us -> 9.7 us
    unnamed x2, blocking collectives: 83.4 us -> 164 us
    all_gather x1 -> x0, waiting for transfers between devices: 48.4 us -> none  [per_device(): lax.all_gather(weight_in, ('dp', 'seq'), axis=0, tiled=True)]
    ppermute x0 -> x5, waiting for transfers between devices: none -> 33.9 us  [collect(): theirs = lax.ppermute(grown, axis, [(d, d ^ reach) for d in range(ways)])]
    all_gather x1, waiting for transfers between devices: 19.7 us -> 0.02 us  [per_device(): lax.all_gather(weight_out, ('dp', 'seq'), axis=0, tiled=True)]
    ppermute x0 -> x5, starting transfers between devices: none -> 9.5 us  [collect(): theirs = lax.ppermute(grown, axis, [(d, d ^ reach) for d in range(ways)])]
    unnamed x50 -> x48, local copies, waits for them, and re-layouts: 14.4 us -> 9.97 us
  transfers between devices with their start and end apart: 6 -> 10, of which waited for: 5 -> 7; matrix products, arithmetic and copies ran while one was open for 17% -> 17% of each run, Pallas kernels for 0% -> 0%
where the time goes in v1:
time: 679 us; the launch traced here: 675 us
  waiting for transfers between devices  315 us (46%)
  blocking collectives  164 us (24%)
  matrix products  93.6 us (14%)
  other arithmetic  59.2 us (9%)
  local copies, waits for them, and re-layouts  18.8 us (3%)
  between operations  14.3 us (2%)
  starting transfers between devices  9.7 us (1%)
    unnamed x2, blocking collectives  164 us
    reduce_scatter x1, waiting for transfers between devices, per_device(): lax.psum_scatter(grad_w_out, ('dp', 'seq'), scatter_dimension=0, tiled=True)  142 us
    reduce_scatter x1, waiting for transfers between devices, per_device(): lax.psum_scatter(grad_w_in, ('dp', 'seq'), scatter_dimension=0, tiled=True)  127 us
    ppermute x5, waiting for transfers between devices, collect(): theirs = lax.ppermute(grown, axis, [(d, d ^ reach) for d in range(ways)])  33.9 us
    convert_element_type x1, other arithmetic, per_device(): act_low = activated.astype(jnp.bfloat16)  32.1 us
    dot_general x1, matrix products, per_device(): jnp.einsum('rkd,fd->rkf', d_branch, full_w_out, preferred_element_type=jn...  18.3 us
    another operation x3, other arithmetic  16.2 us
    dot_general x1, matrix products, per_device(): jnp.einsum('rkd,df->rkf', normed_low, full_w_in, preferred_element_type=j...  14.5 us
  transfers between devices with their start and end apart: 10, of which 7 were waited for; matrix products, arithmetic and copies ran while one was open for 17% of the time, Pallas kernels for 0%

profile of v1, /device:TPU:0, one launch (start us, length us, event | category | flops | bytes accessed | tf_op | source)
XLA Modules:
  0.0 675.2 jit_solution(8503162242583314782)
XLA Ops:
  8.0 3.0 collective-permute-start
  11.0 4.1 collective-permute-done
  16.2 1.6 collective-permute-done.1
  17.9 1.8 collective-permute-start.2
  19.6 13.7 %collective-permute-done.2 = bf16[96,3072]{1,0:T(8,128)(2,1)S(1)} collective-permute-done((bf16[96,3072]{1,0:T(8,128)(2,1)S(1)}, bf16[96,3072]{1,0:T(8,128)(2,1)S(1)}, u32[]{:S(2)}, u32[]{:S(2)}) %collective-permute-start.2) | collective-permute-done | bytes 589856 | tf_op jit(solution)/shard_map/ppermute | solution.py:14
  33.5 1.9 collective-permute-start.3
  35.6 10.8 %negate_convert_fusion = (bf16[768,768]{1,0:T(8,128)(2,1)}, bf16[768,768]{1,0:T(8,128)(2,1)}) fusion(), kind=kLoop, calls=%fused_computation.67 | loop fusion | flops 8257536 | bytes 2359296 | tf_op jit(solution)/shard_map/convert.3
  46.3 14.6 %collective-permute-done.3 = bf16[192,3072]{1,0:T(8,128)(2,1)S(1)} collective-permute-done((bf16[192,3072]{1,0:T(8,128)(2,1)S(1)}, bf16[192,3072]{1,0:T(8,128)(2,1)S(1)}, u32[]{:S(2)}, u32[]{:S(2)}) %collective-permute-start.3) | collective-permute-done | bytes 1179680 | tf_op jit(solution)/shard_map/ppermute | solution.py:14
  61.0 1.8 maximum_select_fusion.1
  62.8 2.8 collective-permute-start.4
  67.0 124.8 %all-reduce.13 = (bf16[768]{0:T(1024)(128)(2,1)S(1)}, bf16[768]{0:T(1024)(128)(2,1)S(1)}, bf16[3072]{0:T(1024)(128)(2,1)S(1)}, bf16[768]{0:T(1024)(128)(2,1)S(1)...) all-reduce(bf16[768]{0:T(1024)(128)(2,1)S(1)} %dynamic-update-slice, ...), channel_id=1, replica_groups=mesh['dp'=16,'seq'=2] {'dp','seq'}, use_global_device_ids=true, to_apply=%add.1 | all-reduce | flops 6912 | bytes 27648
  191.9 2.5 multiply_convert_fusion.5
  194.4 4.1 convert_bitcast_fusion
  200.6 2.8 fusion.67
  203.9 14.5 %fusion.19 = (u8[256,3072]{1,0:T(8,128)(4,1)S(1)}, u8[256,3072]{1,0:T(8,128)(4,1)S(1)}, f32[4,256,3072]{2,1,0:T(8,128)}) fusion(f32[3072]{0:T(1024)S(1)} %convert_element_type.83, bf16[384,3072]{1,0:T(8,128)(2,1)} %collective-permute-done.4, bf16[384,3072]{1,0:T(8,128)(2,1)} %maximum_select_fusion.1, pred[]{:T(512)S(6)} %eq.21, ...), kind=kOutput, calls=%fused_computation.56 | convolution fusion | flops 4899471360 | bytes 22046720 | tf_op jit(solution)/shard_map/rkd,df->rkf/dot_general | solution.py:89
  218.4 32.1 %multiply_convert_fusion = (bf16[4,256,3072]{2,1,0:T(8,128)(2,1)}, f32[4,256,3072]{2,1,0:T(8,128)}) fusion(f32[4,256,3072]{2,1,0:T(8,128)} %get-tuple-element.49, f32[3072]{0:T(1024)S(1)} %convert_element_type.83, u8[256,3072]{1,0:T(8,128)(4,1)S(1)} %get-tuple-element.11, u8[256,3072]{1,0:T(8,128)(4,1)S(1)} %get-tuple-element.10), kind=kLoop, calls=%fused_computation.9 | loop fusion | flops 223346688 | bytes 33042432 | tf_op jit(solution)/shard_map/convert_element_type | solution.py:93
  250.6 8.9 %fusion.68 = (f32[4,256]{1,0:T(4,128)S(1)}, f32[4,256,768]{2,1,0:T(8,128)S(1)}) fusion(f32[768]{0:T(1024)S(1)} %convert_element_type.85, bf16[4,256,3072]{2,1,0:T(8,128)(2,1)} %get-tuple-element.36, bf16[3072,768]{1,0:T(8,128)(2,1)} %all-gather.6.cloned.1.call-done, f32[768]{0:T(1024)S(1)} %convert_element_type.81, f32[768]{0:T(1024)S(1)} %convert_element_type.80, ...), kind=kOutput, calls=%fused_computation.126 | convolution fusion | flops 4837342208 | bytes 17323008 | tf_op jit(solution)/shard_map/rkf,fd->rkd/dot_general | solution.py:94
  260.9 1.8 fusion.13
  262.7 2.7 convert_reduce_fusion.2
  265.5 18.3 %convert_reduce_fusion = (f32[3072]{0:T(1024)S(1)}, bf16[4,256,3072]{2,1,0:T(8,128)(2,1)}) fusion(f32[4,256,3072]{2,1,0:T(8,128)} %get-tuple-element.37, bf16[4,256,768]{2,1,0:T(8,128)(2,1)} %get-tuple-element.33, bf16[3072,768]{1,0:T(8,128)(2,1)} %all-gather.6.cloned.1.call-done, f32[4,256,3072]{2,1,0:T(8,128)} %get-tuple-element.49, ...), kind=kOutput, calls=%fused_computation.7 | convolution fusion | flops 4885312512 | bytes 37773312 | tf_op jit(solution)/shard_map/rkd,fd->rkf/dot_general | solution.py:102
  283.8 12.2 %multiply_reduce_fusion = (f32[768]{0:T(1024)S(1)}, f32[4,256]{1,0:T(4,128)S(1)}, f32[768]{0:T(1024)S(1)}, f32[4,256,768]{2,1,0:T(8,128)S(1)}) fusion(f32[4,256,768]{2,1,0:T(8,128)S(1)} %get-tuple-element.48, f32[4,256]{1,0:T(4,128)S(1)} %fusion.55, f32[4,256]{1,0:T(4,128)S(1)} %broadcast_multiply_fusion.1, f32[768]{0:T(1024)S(1)} %convert_element_type.80, ...), kind=kOutput, calls=%fused_computation.46 | convolution fusion | flops 4866438144 | bytes 22061056 | tf_op jit(solution)/shard_map/rkf,df->rkd/dot_general | solution.py:107
  297.2 1.6 copy-done.1
  298.9 5.0 convolution_convert_fusion
  304.0 10.6 %convolution_bitcast_fusion.1 = f32[768,3072]{1,0:T(8,128)} fusion(bf16[4,256,3072]{2,1,0:T(8,128)(2,1)} %get-tuple-element.54, f32[4,256,768]{2,1,0:T(8,128)S(1)} %get-tuple-element.48, f32[768]{0:T(1024)S(1)} %convert_element_type.81, f32[768]{0:T(1024)S(1)} %convert_element_type.80, f32[4,256]{1,0:T(4,128)S(1)} %fusion.55, ...), kind=kOutput, calls=%fused_computation.23 | convolution fusion | flops 4835770368 | bytes 18888704 | tf_op jit(solution)/shard_map/rkd,rkf->df/dot_general | solution.py:105
  316.1 10.9 %convolution_bitcast_fusion = f32[3072,768]{1,0:T(8,128)} fusion(bf16[4,256,3072]{2,1,0:T(8,128)(2,1)} %get-tuple-element.36, bf16[4,256,768]{2,1,0:T(8,128)(2,1)S(1)} %copy-done.4), kind=kOutput, calls=%fused_computation.22 | convolution fusion | flops 4831838208 | bytes 17301504 | tf_op jit(solution)/shard_map/rkf,rkd->fd/dot_general | solution.py:100
  327.1 3.0 multiply_convert_fusion.3
  330.0 39.4 %all-reduce.12 = (f32[3072]{0:T(1024)S(1)}, f32[768]{0:T(1024)S(1)}, f32[768]{0:T(1024)S(1)}, f32[768]{0:T(1024)S(1)}, f32[768]{0:T(1024)S(1)}, /*index=5*/f32[768]{0:T(1024)S(1)}) all-reduce(f32[3072]{0:T(1024)S(1)} %get-tuple-element.53, f32[768]{0:T(1024)S(1)} %get-tuple-element.32, ...), channel_id=3, replica_groups=mesh['dp'=16,'seq'=2] {'dp','seq'}, use_global_device_ids=true, to_apply=%region_10.11.clone | all-reduce | flops 6912 | bytes 55296
  372.9 11.8 %all-gather.8.cloned.1.call-done = bf16[4,512,1536]{2,1,0:T(8,128)(2,1)} async-done(((bf16[4,256,1536]{2,1,0:T(8,128)(2,1)}), bf16[4,512,1536]{2,1,0:T(8,128)(2,1)}) %all-gather.8.cloned.1.call-update) | async-done | bytes 6291472 | tf_op jit(solution)/shard_map/all_gather | solution.py:115
  384.7 8.6 %copy.31 = bf16[4,512,1536]{1,2,0:T(8,128)(2,1)} copy(bf16[4,512,1536]{2,1,0:T(8,128)(2,1)} %all-gather.8.cloned.1.call-done) | data formatting | bytes 12582912 | tf_op jit(solution)/shard_map/reshape | solution.py:119
  393.3 6.3 bitcast_add_fusion
  399.6 126.8 %reduce-scatter.3.cloned.1.call-done = f32[24,3072]{1,0:T(8,128)} async-done(((f32[768,3072]{1,0:T(8,128)}), f32[24,3072]{1,0:T(8,128)}) %reduce-scatter.3.cloned.1.call-update) | async-done | bytes 294928 | tf_op jit(solution)/shard_map/reduce_scatter | solution.py:123
  526.5 142.0 %reduce-scatter.5.cloned.1.call-done = f32[96,768]{1,0:T(8,128)} async-done(((f32[3072,768]{1,0:T(8,128)}), f32[96,768]{1,0:T(8,128)}) %reduce-scatter.5.cloned.1.call-update) | async-done | bytes 294928 | tf_op jit(solution)/shard_map/reduce_scatter | solution.py:125
  (82 shorter events, 14.1 us)
Async XLA Ops:
  7.2 187.2 %all-gather.4.cloned.1.call-start = ((), (), s32[]{:S(2)}) async-start(), calls=%async_computation.2 | async-start | bytes 4718592 | tf_op jit(solution)/shard_map/all_gather | solution.py:76
  7.9 242.6 %all-gather.6.cloned.1.call-start = ((), (), s32[]{:S(2)}) async-start(), calls=%async_computation.3 | async-start | bytes 4866048 | tf_op jit(solution)/shard_map/all_gather | solution.py:56
  8.0 7.1 %collective-permute-start = (bf16[24,3072]{1,0:T(8,128)(2,1)}, bf16[24,3072]{1,0:T(8,128)(2,1)S(1)}, u32[]{:S(2)}, u32[]{:S(2)}) collective-permute-start(bf16[24,3072]{1,0:T(8,128)(2,1)} %param.11), channel_id=1, source_target_pairs={{0,1},{1,0},{2,3},{3,2},{4,5},{5,4},{6,7},{7,6},{8,9},{9,8},{10,11... | collective-permute-start | bytes 442376 | tf_op jit(solution)/shard_map/ppermute | solution.py:14
  16.1 1.6 collective-permute-start.1
  17.9 15.4 %collective-permute-start.2 = (bf16[96,3072]{1,0:T(8,128)(2,1)S(1)}, bf16[96,3072]{1,0:T(8,128)(2,1)S(1)}, u32[]{:S(2)}, u32[]{:S(2)}) collective-permute-start(bf16[96,3072]{1,0:T(8,128)(2,1)S(1)} %maximum_select_fusion.3), channel_id=1, source_target_pairs={{0,4},{1,5},{2,6},{3,7},{4,0},{5,1},{6,2},{7,3},{8,12},{9,13},{10,... | collective-permute-start | bytes 1769480 | tf_op jit(solution)/shard_map/ppermute | solution.py:14
  33.5 27.4 %collective-permute-start.3 = (bf16[192,3072]{1,0:T(8,128)(2,1)S(1)}, bf16[192,3072]{1,0:T(8,128)(2,1)S(1)}, u32[]{:S(2)}, u32[]{:S(2)}) collective-permute-start(bf16[192,3072]{1,0:T(8,128)(2,1)S(1)} %maximum_select_fusion.2), channel_id=1, source_target_pairs={{0,8},{1,9},{2,10},{3,11},{4,12},{5,13},{6,14},{7,15},{8,0},{9,1},... | collective-permute-start | bytes 3538952 | tf_op jit(solution)/shard_map/ppermute | solution.py:14
  35.4 349.3 %all-gather.8.cloned.1.call-start = ((), (), s32[]{:S(2)}) async-start(), calls=%async_computation.4 | async-start | bytes 9437184 | tf_op jit(solution)/shard_map/all_gather | solution.py:115
  35.5 30.1 %copy-start.9 = (bf16[24]{0:T(256)(128)(2,1)S(1)}, bf16[24]{0:T(256)(128)(2,1)}, u32[]{:S(2)}) copy-start(bf16[24]{0:T(256)(128)(2,1)} %param.16) | copy-start | bytes 148
  35.5 30.3 %copy-start.10 = (bf16[24]{0:T(256)(128)(2,1)S(1)}, bf16[24]{0:T(256)(128)(2,1)}, u32[]{:S(2)}) copy-start(bf16[24]{0:T(256)(128)(2,1)} %param.15) | copy-start | bytes 148
  35.5 30.5 %copy-start.11 = (bf16[24]{0:T(256)(128)(2,1)S(1)}, bf16[24]{0:T(256)(128)(2,1)}, u32[]{:S(2)}) copy-start(bf16[24]{0:T(256)(128)(2,1)} %param.14) | copy-start | bytes 148
  35.5 30.7 %copy-start.12 = (bf16[24]{0:T(256)(128)(2,1)S(1)}, bf16[24]{0:T(256)(128)(2,1)}, u32[]{:S(2)}) copy-start(bf16[24]{0:T(256)(128)(2,1)} %param.18) | copy-start | bytes 148
  35.5 31.0 %copy-start.13 = (bf16[24]{0:T(256)(128)(2,1)S(1)}, bf16[24]{0:T(256)(128)(2,1)}, u32[]{:S(2)}) copy-start(bf16[24]{0:T(256)(128)(2,1)} %param.17) | copy-start | bytes 148
  35.5 31.2 %copy-start.14 = (bf16[96]{0:T(256)(128)(2,1)S(1)}, bf16[96]{0:T(256)(128)(2,1)}, u32[]{:S(2)}) copy-start(bf16[96]{0:T(256)(128)(2,1)} %param.12) | copy-start | bytes 580
  62.8 141.1 %collective-permute-start.4 = (bf16[384,3072]{1,0:T(8,128)(2,1)}, bf16[384,3072]{1,0:T(8,128)(2,1)}, u32[]{:S(2)}, u32[]{:S(2)}) collective-permute-start(bf16[384,3072]{1,0:T(8,128)(2,1)} %maximum_select_fusion.1), channel_id=1, source_target_pairs={{0,16},{1,17},{2,18},{3,19},{4,20},{5,21},{6,22},{7,23},{8,24},{9,... | collective-permute-start | bytes 7077896 | tf_op jit(solution)/shard_map/ppermute | solution.py:14
  198.5 1.4 copy-start.3
  198.5 1.8 copy-start.5
  198.5 2.1 copy-start.7
  250.5 8.9 %copy-start = (bf16[4,256,768]{2,1,0:T(8,128)(2,1)S(1)}, bf16[4,256,768]{2,1,0:T(8,128)(2,1)}, u32[]{:S(2)}) copy-start(bf16[4,256,768]{2,1,0:T(8,128)(2,1)} %param.19) | copy-start | bytes 4718596
  296.0 2.9 copy-start.6
  296.0 2.9 copy-start.8
  297.2 1.7 copy-start.1
  303.9 222.6 %reduce-scatter.3.cloned.1.call-start = ((), (), s32[]{:S(2)}) async-start(), calls=%async_computation.5 | async-start | bytes 9732096 | tf_op jit(solution)/shard_map/reduce_scatter | solution.py:123
  314.6 1.5 copy-start.4
  314.6 353.8 %reduce-scatter.5.cloned.1.call-start = ((), (), s32[]{:S(2)}) async-start(), calls=%async_computation.6 | async-start | bytes 9732096 | tf_op jit(solution)/shard_map/reduce_scatter | solution.py:125
  372.9 20.4 %copy-start.2 = (f32[4,256,768]{2,1,0:T(8,128)S(1)}, f32[4,256,768]{2,1,0:T(8,128)}, u32[]{:S(2)}) copy-start(f32[4,256,768]{2,1,0:T(8,128)} %copy-done.1) | copy-start | bytes 9437188
Sparse Core Ops, SparseCore 0:
  9.6 47.6 all-gather.3
  60.1 155.1 all-gather.5
  304.0 80.6 all-gather.7
  391.1 135.3 reduce-scatter.2
  533.8 134.5 reduce-scatter.4
